TPU v7x, 512 devices: a whole 4x8x8 slice. The times are simulated.
512 devices in a mesh: ctx: 32 (over x_hi, y, core), batch: 16 (over z, x_lo).
Axes of the slice: x: 4 (x_hi: 2, x_lo: 2; x = x_hi * 2 + x_lo), y: 8, z: 8, core: 2. Of those that a mesh axis runs over, the one named last changes fastest.
Arguments:
- seq_in: bfloat16 [16, 4096, 512], P('batch', 'ctx'), may hold values from -6 to 6
- w_in: bfloat16 [512, 2048], replicated, may hold values from -0.25 to 0.25
- w_out: bfloat16 [512, 512], replicated, may hold values from -0.25 to 0.25
- pos_emb: bfloat16 [16, 4096, 512], P('batch', 'ctx'), may hold values from -0.29882812 to 0.29882812
- pos_ids: int32 [16, 4096], P('batch', 'ctx'), may hold values from 0 to 3999999, as said below
- neg_emb: bfloat16 [128, 512], P('batch'), may hold values from -0.29882812 to 0.29882812
- neg_ids: int32 [128], P('batch'), may hold values from 0 to 3999999
- neg_counts: int32 [128], P('batch'), may hold values from 1000 to 99999
Outputs:
- loss: float32 [16, 4096], P('batch', 'ctx')
- d_seq: bfloat16 [16, 4096, 512], P('batch', 'ctx')
- d_neg: float32 [128, 512], P('batch')
Inputs may be any that keep to these rules, and one draw needn't show every extreme that they name: `pos_ids`: item ids; many positions name the item of one of the sampled negatives.
All inputs are finite; a program needn't handle non-finite values.
Results may differ from a plain program's by a relative error of at most 0.008.
Values may be sent and summed in bfloat16 or wider, within the bound.
A program may use at most 128 MiB of HBM per device.

v0:
```python
import math
import jax
import jax.numpy as jnp
from jax import lax
from jax.sharding import PartitionSpec as P

HEADS = 8
HEAD = 64
D = 512
SOFTMAX_TEMPER = 0.05


def silu_slope(scores):
    sigma = jax.nn.sigmoid(scores)
    return sigma * (1.0 + scores * (1.0 - sigma))


def split_heads(matrix):
    return matrix.reshape(matrix.shape[0], HEADS, HEAD)


def shards(seq_in, w_in, w_out, pos_emb, pos_ids, neg_emb, neg_ids, neg_counts):
    tokens = seq_in.shape[1]
    score_scale = HEAD ** (-0.5)
    offset = lax.axis_index("ctx") * tokens
    row_pos = offset + lax.iota(jnp.int32, tokens)
    neg_float = neg_emb.astype(jnp.float32)
    neg_scale = lax.rsqrt(jnp.sum(neg_float * neg_float, axis=1, keepdims=True) + 1e-06)
    neg_unit = neg_float * neg_scale
    every_unit_vector, all_ids, all_counts = (
        lax.all_gather(neg_unit.astype(jnp.bfloat16), "batch", axis=0, tiled=True),
        lax.all_gather(neg_ids, "batch", axis=0, tiled=True),
        lax.all_gather(neg_counts, "batch", axis=0, tiled=True),
    )
    count_float = all_counts.astype(jnp.float32)
    log_sample_share = jnp.log(all_counts.shape[0] * count_float / jnp.sum(count_float))
    seq_x = seq_in[0]
    pre_act = jnp.dot(seq_x, w_in, preferred_element_type=jnp.float32)
    proj = jax.nn.silu(pre_act).astype(jnp.bfloat16)
    gate_u = proj[:, :D].astype(jnp.float32)
    value_rows = proj[:, D : 2 * D]
    query_rows = proj[:, 2 * D : 3 * D]
    key_rows = proj[:, 3 * D :]
    all_values, all_keys = (
        lax.all_gather(value_rows, "ctx", axis=0, tiled=True),
        lax.all_gather(key_rows, "ctx", axis=0, tiled=True),
    )
    length = all_keys.shape[0]
    block_rows = math.gcd(length, 512)
    heads_keys = split_heads(all_keys)
    heads_values = split_heads(all_values)
    local_q = split_heads(query_rows)
    local_k = split_heads(key_rows)
    local_v = split_heads(value_rows)
    empty = jnp.zeros((tokens, HEADS, HEAD), jnp.float32)

    def forward_step(index, carry):
        start = index * block_rows
        keys_blk = lax.dynamic_slice_in_dim(heads_keys, start, block_rows, 0)
        values_blk = lax.dynamic_slice_in_dim(heads_values, start, block_rows, 0)
        scores = (
            jnp.einsum("ihe,jhe->hij", local_q, keys_blk, preferred_element_type=jnp.float32)
            * score_scale
        )
        allowed = ((start + lax.iota(jnp.int32, block_rows))[None, :] <= row_pos[:, None])[None]
        weights = jnp.where(allowed, jax.nn.silu(scores), 0.0).astype(jnp.bfloat16)
        return carry + jnp.einsum(
            "hij,jhe->ihe", weights, values_blk, preferred_element_type=jnp.float32
        )

    mixed = lax.fori_loop(0, length // block_rows, forward_step, empty).reshape(tokens, D)
    centred = mixed - jnp.mean(mixed, axis=1, keepdims=True)
    inv_std = lax.rsqrt(jnp.mean(centred * centred, axis=1, keepdims=True) + 1e-05)
    normed = centred * inv_std
    gated = (normed * gate_u).astype(jnp.bfloat16)
    outputs = seq_x.astype(jnp.float32) + jnp.dot(gated, w_out, preferred_element_type=jnp.float32)
    out_scale = lax.rsqrt(jnp.sum(outputs * outputs, axis=1, keepdims=True) + 1e-06)
    user_vector = outputs * out_scale
    user_rounded = user_vector.astype(jnp.bfloat16)
    pos_float = pos_emb[0].astype(jnp.float32)
    positive_unit = pos_float * lax.rsqrt(
        jnp.sum(pos_float * pos_float, axis=1, keepdims=True) + 1e-06
    )
    positive_item = jnp.sum(user_vector * positive_unit, axis=1) / SOFTMAX_TEMPER
    score_logits = (
        jnp.einsum("id,nd->in", user_rounded, every_unit_vector, preferred_element_type=jnp.float32)
        / SOFTMAX_TEMPER
        - log_sample_share[None, :]
    )
    allowed_items = pos_ids[0][:, None] != all_ids[None, :]
    terms = jnp.where(allowed_items, jnp.exp(score_logits), 0.0)
    pos_exp = jnp.exp(positive_item)
    denom = pos_exp + jnp.sum(terms, axis=1)
    loss = jnp.log(denom) - positive_item
    positive_gradient = pos_exp / denom - 1.0
    probabilities = (terms / denom[:, None]).astype(jnp.bfloat16)
    user_gradient = (
        positive_gradient[:, None] * positive_unit / SOFTMAX_TEMPER
        + jnp.dot(probabilities, every_unit_vector, preferred_element_type=jnp.float32)
        / SOFTMAX_TEMPER
    )
    unit_gradient = (
        jnp.einsum("wz,wb->zb", probabilities, user_rounded, preferred_element_type=jnp.float32)
        / SOFTMAX_TEMPER
    )
    owned = lax.psum_scatter(
        unit_gradient.astype(jnp.bfloat16), "batch", scatter_dimension=0, tiled=True
    ).astype(jnp.float32)
    d_total = lax.psum(owned, "ctx")
    d_neg = neg_scale * (d_total - neg_unit * jnp.sum(neg_unit * d_total, axis=1, keepdims=True))
    d_outputs = out_scale * (
        user_gradient - user_vector * jnp.sum(user_vector * user_gradient, axis=1, keepdims=True)
    )
    d_gated = jnp.einsum(
        "ik,dk->id", d_outputs.astype(jnp.bfloat16), w_out, preferred_element_type=jnp.float32
    )
    d_normed = d_gated * gate_u
    d_gate = d_gated * normed
    d_mixed = inv_std * (
        d_normed
        - jnp.mean(d_normed, axis=1, keepdims=True)
        - normed * jnp.mean(d_normed * normed, axis=1, keepdims=True)
    )
    d_rows = d_mixed.astype(jnp.bfloat16)
    d_heads = split_heads(d_rows)

    def query_step(index, carry):
        start = index * block_rows
        keys_blk = lax.dynamic_slice_in_dim(heads_keys, start, block_rows, 0)
        values_blk = lax.dynamic_slice_in_dim(heads_values, start, block_rows, 0)
        scores = (
            jnp.einsum("ihe,jhe->hij", local_q, keys_blk, preferred_element_type=jnp.float32)
            * score_scale
        )
        allowed = ((start + lax.iota(jnp.int32, block_rows))[None, :] <= row_pos[:, None])[None]
        d_weights = jnp.einsum(
            "ihe,jhe->hij", d_heads, values_blk, preferred_element_type=jnp.float32
        )
        d_scores = jnp.where(allowed, d_weights * silu_slope(scores) * score_scale, 0.0).astype(
            jnp.bfloat16
        )
        return carry + jnp.einsum(
            "hij,jhe->ihe", d_scores, keys_blk, preferred_element_type=jnp.float32
        )

    d_queries = lax.fori_loop(0, length // block_rows, query_step, empty)
    queries_piece = lax.all_gather(query_rows, "ctx", axis=0, tiled=True)
    grads_piece = lax.all_gather(d_rows, "ctx", axis=0, tiled=True)
    count = queries_piece.shape[0]
    inner = math.gcd(count, 512)

    def inner_step(index, sums):
        first = index * inner
        query_blk = split_heads(lax.dynamic_slice_in_dim(queries_piece, first, inner, 0))
        grad_blk = split_heads(lax.dynamic_slice_in_dim(grads_piece, first, inner, 0))
        query_pos = first + lax.iota(jnp.int32, inner)
        scores = (
            jnp.einsum("ihe,jhe->hij", query_blk, local_k, preferred_element_type=jnp.float32)
            * score_scale
        )
        allowed = (row_pos[None, :] <= query_pos[:, None])[None]
        weights = jnp.where(allowed, jax.nn.silu(scores), 0.0).astype(jnp.bfloat16)
        d_weights = jnp.einsum(
            "ihe,jhe->hij", grad_blk, local_v, preferred_element_type=jnp.float32
        )
        d_scores = jnp.where(allowed, d_weights * silu_slope(scores) * score_scale, 0.0).astype(
            jnp.bfloat16
        )
        new_keys = sums[0] + jnp.einsum(
            "hij,ihe->jhe", d_scores, query_blk, preferred_element_type=jnp.float32
        )
        new_values = sums[1] + jnp.einsum(
            "hij,ihe->jhe", weights, grad_blk, preferred_element_type=jnp.float32
        )
        return (new_keys, new_values)

    d_keys, d_values = lax.fori_loop(0, count // inner, inner_step, (empty, empty))
    d_proj = jnp.concatenate(
        [
            d_gate,
            d_values.reshape(tokens, D),
            d_queries.reshape(tokens, D),
            d_keys.reshape(tokens, D),
        ],
        axis=1,
    )
    d_pre = (d_proj * silu_slope(pre_act)).astype(jnp.bfloat16)
    d_seq = (
        d_outputs + jnp.einsum("ik,dk->id", d_pre, w_in, preferred_element_type=jnp.float32)
    ).astype(jnp.bfloat16)
    return (loss[None], d_seq[None], d_neg)


def solution(mesh):
    in_specs = (
        P("batch", "ctx", None),
        P(),
        P(),
        P("batch", "ctx", None),
        P("batch", "ctx"),
        P("batch", None),
        P("batch"),
        P("batch"),
    )
    out_specs = (P("batch", "ctx"), P("batch", "ctx", None), P("batch", None))
    return jax.shard_map(shards, mesh=mesh, in_specs=in_specs, out_specs=out_specs, check_vma=False)
```

profile of v0, /device:TPU:1, one launch (start us, length us, event | category | flops | bytes accessed | tf_op | source)
XLA Modules:
  0.0 607.7 jit_solution(220923983265694282)
XLA Ops:
  15.3 19.5 %all-reduce.2 = (s32[128]{0:T(128)S(1)}, s32[128]{0:T(128)}) all-reduce(s32[128]{0:T(128)S(1)} %dynamic-update-slice.1, s32[128]{0:T(128)S(1)} %dynamic-update-slice), channel_id=1, replica_groups=mesh['ctx'=32,'batch'=16] {'batch'}, use_global_device_ids=true, to_apply=%add.1 | all-reduce | flops 256 | bytes 2048
  35.0 26.8 %all_gather.24 = bf16[128,512]{1,0:T(8,128)(2,1)} all-gather(bf16[8,512]{1,0:T(8,128)(2,1)S(1)} %fusion.98), channel_id=1, replica_groups=mesh['ctx'=32,'batch'=16] {'batch'}, dimensions={0}, use_global_device_ids=true | all-gather | bytes 139264 | tf_op jit(solution)/shard_map/all_gather | solution.py:31
  64.2 45.5 %all-gather.5.cloned.1.call-done = bf16[4096,512]{1,0:T(8,128)(2,1)} async-done(((bf16[128,512]{1,0:T(8,128)(2,1)}), bf16[4096,512]{1,0:T(8,128)(2,1)}) %all-gather.5.cloned.1.call-update) | async-done | bytes 4194320 | tf_op jit(solution)/shard_map/all_gather | solution.py:45
  109.7 6.4 %copy.27 = bf16[4096,512]{0,1:T(8,128)(2,1)} copy(bf16[4096,512]{1,0:T(8,128)(2,1)} %all-gather.5.cloned.1.call-done) | data formatting | bytes 8388608 | tf_op jit(solution)/shard_map/all_gather | solution.py:45
  116.1 86.6 %all-gather.7.cloned.1.call-done = bf16[4096,512]{1,0:T(8,128)(2,1)} async-done(((bf16[128,512]{1,0:T(8,128)(2,1)}), bf16[4096,512]{1,0:T(8,128)(2,1)}) %all-gather.7.cloned.1.call-update) | async-done | bytes 4194320 | tf_op jit(solution)/shard_map/all_gather | solution.py:46
  202.7 6.4 %copy.28 = bf16[4096,512]{0,1:T(8,128)(2,1)} copy(bf16[4096,512]{1,0:T(8,128)(2,1)} %all-gather.7.cloned.1.call-done) | data formatting | bytes 8388608 | tf_op jit(solution)/shard_map/all_gather | solution.py:46
  209.1 19.7 %while.44 = (s32[]{:T(128)}, f32[128,8,64]{0,2,1:T(8,128)S(1)}, bf16[4096,8,64]{0,2,1:T(8,128)(2,1)}, bf16[4096,8,64]{0,2,1:T(8,128)(2,1)}, bf16[128,8,64]{0,2,1...) while((s32[]{:T(128)}, f32[128,8,64]{0,2,1:T(8,128)S(1)}, ...), condition=%wide.region_1.0_spmd.clone, body=%wide.region_0.0_spmd.clone.sunk | while | flops 138084992 | bytes 1841828 | solution.py:71
  245.2 57.4 %while.46 = (s32[]{:T(128)}, f32[128,8,64]{0,2,1:T(8,128)}, bf16[4096,8,64]{0,2,1:T(8,128)(2,1)}, bf16[4096,8,64]{0,2,1:T(8,128)(2,1)}, bf16[128,8,64]{2,1,0:T(8...) while((s32[]{:T(128)}, f32[128,8,64]{0,2,1:T(8,128)}, ...), condition=%wide.region_16.17_spmd.clone, body=%wide.region_15.16_spmd.clone.sunk | while | flops 207815296 | bytes 9313028 | solution.py:146
  248.3 3.3 fusion.162
  255.5 3.3 fusion.162
  262.6 3.4 fusion.162
  269.8 3.4 fusion.162
  277.0 3.4 fusion.162
  284.2 3.3 fusion.162
  291.3 3.3 fusion.162
  298.5 3.3 fusion.162
  304.9 125.1 %psum.7 = f32[8,512]{1,0:T(8,128)S(1)} all-reduce(bf16[8,512]{1,0:T(8,128)(2,1)} %reduce-scatter.2.cloned.1.call-done), channel_id=1, replica_groups=mesh['ctx'=32,'batch'=16] {'ctx'}, use_global_device_ids=true, to_apply=%region_18.19 | all-reduce | flops 4096 | bytes 24576 | tf_op jit(solution)/shard_map/psum | solution.py:109
  430.8 61.0 %all-gather.11.cloned.1.call-done = bf16[4096,512]{1,0:T(8,128)(2,1)} async-done(((bf16[128,512]{1,0:T(8,128)(2,1)}), bf16[4096,512]{1,0:T(8,128)(2,1)}) %all-gather.11.cloned.1.call-update) | async-done | bytes 4194320 | tf_op jit(solution)/shard_map/all_gather | solution.py:148
  491.8 104.2 %while.45 = (s32[]{:T(128)}, f32[128,8,64]{0,2,1:T(8,128)}, f32[128,8,64]{0,2,1:T(8,128)}, bf16[4096,512]{1,0:T(8,128)(2,1)}, bf16[4096,512]{1,0:T(8,128)(2,1)},...) while((s32[]{:T(128)}, f32[128,8,64]{0,2,1:T(8,128)}, ...), condition=%wide.region_14.15_spmd.clone, body=%wide.region_13.14_spmd.clone.sunk | while | flops 278725248 | bytes 16192726 | solution.py:177
  501.2 3.6 fusion.154
  514.1 3.7 fusion.154
  524.0 3.1 fusion.155
  527.1 3.7 fusion.154
  537.0 3.1 fusion.155
  540.2 3.7 fusion.154
  550.1 3.1 fusion.155
  553.2 3.7 fusion.154
  563.1 3.1 fusion.155
  566.3 3.7 fusion.154
  579.3 3.7 fusion.154
  589.2 3.1 fusion.155
  592.3 3.7 fusion.154
  (295 shorter events, 142.6 us)
Async XLA Ops:
  7.2 7.6 %copy-start.27 = (s32[8]{0:T(128)S(1)}, s32[8]{0:T(128)}, u32[]{:S(2)}) copy-start(s32[8]{0:T(128)} %param.20) | copy-start | bytes 100
  7.2 7.9 %copy-start.28 = (s32[8]{0:T(128)S(1)}, s32[8]{0:T(128)}, u32[]{:S(2)}) copy-start(s32[8]{0:T(128)} %param.21) | copy-start | bytes 100
  7.2 27.6 %copy-start.15 = (bf16[8,512]{1,0:T(8,128)(2,1)S(1)}, bf16[8,512]{1,0:T(8,128)(2,1)}, u32[]{:S(2)}) copy-start(bf16[8,512]{1,0:T(8,128)(2,1)} %param.19) | copy-start | bytes 24580
  7.2 55.1 %copy-start.3 = (bf16[1,128,512]{2,1,0:T(8,128)(2,1)S(1)}, bf16[1,128,512]{2,1,0:T(8,128)(2,1)}, u32[]{:S(2)}) copy-start(bf16[1,128,512]{2,1,0:T(8,128)(2,1)} %param.17) | copy-start | bytes 393220
  7.2 102.5 %all-gather.5.cloned.1.call-start = ((), (), s32[]{:S(2)}) async-start(), calls=%async_computation.1 | async-start | bytes 4325376 | tf_op jit(solution)/shard_map/all_gather | solution.py:45
  11.9 104.2 %copy-start.5 = (bf16[128,512]{1,0:T(8,128)(2,1)}, bf16[128,512]{1,0:T(8,128)(2,1)S(1)}, u32[]{:S(2)}) copy-start(bf16[128,512]{1,0:T(8,128)(2,1)S(1)} %get-tuple-element.547) | copy-start | bytes 393220
  11.9 190.8 %all-gather.7.cloned.1.call-start = ((), (), s32[]{:S(2)}) async-start(), calls=%async_computation.2 | async-start | bytes 4325376 | tf_op jit(solution)/shard_map/all_gather | solution.py:46
  12.7 292.2 %reduce-scatter.2.cloned.1.call-start = ((), (), s32[]{:S(2)}) async-start(), calls=%async_computation.5 | async-start | bytes 139264 | tf_op jit(solution)/shard_map/reduce_scatter | solution.py:106
  34.9 81.2 %copy-start.19 = (f32[8]{0:T(128)}, f32[8]{0:T(128)S(1)}, u32[]{:S(2)}) copy-start(f32[8]{0:T(128)S(1)} %add_rsqrt_fusion) | copy-start | bytes 100
  209.1 20.5 %copy-start.2 = (bf16[512,512]{1,0:T(8,128)(2,1)S(1)}, bf16[512,512]{1,0:T(8,128)(2,1)}, u32[]{:S(2)}) copy-start(bf16[512,512]{1,0:T(8,128)(2,1)} %param.16) | copy-start | bytes 1572868
  229.6 10.5 %copy-start.4 = (bf16[1,128,512]{2,1,0:T(8,128)(2,1)S(1)}, bf16[1,128,512]{2,1,0:T(8,128)(2,1)}, u32[]{:S(2)}) copy-start(bf16[1,128,512]{2,1,0:T(8,128)(2,1)} %param.17) | copy-start | bytes 393220
  229.6 10.5 %copy-start.7 = (bf16[128,512]{1,0:T(8,128)(2,1)S(1)}, bf16[128,512]{1,0:T(8,128)(2,1)}, u32[]{:S(2)}) copy-start(bf16[128,512]{1,0:T(8,128)(2,1)} %all_gather.24) | copy-start | bytes 393220
  235.0 195.9 %all-gather.9.cloned.1.call-start = ((), (), s32[]{:S(2)}) async-start(), calls=%async_computation.3 | async-start | bytes 4325376 | tf_op jit(solution)/shard_map/all_gather | solution.py:147
  235.5 256.3 %all-gather.11.cloned.1.call-start = ((), (), s32[]{:S(2)}) async-start(), calls=%async_computation.4 | async-start | bytes 4325376 | tf_op jit(solution)/shard_map/all_gather | solution.py:148
  241.2 3.2 copy-start.9
  241.3 3.2 copy-start.21
  245.1 59.2 %copy-start.24 = (f32[128]{0:T(128)S(1)}, f32[128]{0:T(128)}, u32[]{:S(2)}) copy-start(f32[128]{0:T(128)} %copy-done.23) | copy-start | bytes 1540
  245.2 59.2 %copy-start.26 = (f32[128]{0:T(128)S(1)}, f32[128]{0:T(128)}, u32[]{:S(2)}) copy-start(f32[128]{0:T(128)} %copy-done.25) | copy-start | bytes 1540
  245.2 184.8 %copy-start.20 = (f32[8]{0:T(128)S(1)}, f32[8]{0:T(128)}, u32[]{:S(2)}) copy-start(f32[8]{0:T(128)} %copy-done.19) | copy-start | bytes 100
  245.2 3.1 copy-start.11
  245.2 3.1 copy-start.14
  252.4 3.1 copy-start.14
  259.5 3.1 copy-start.14
  491.8 106.4 %copy-start.22 = (f32[128]{0:T(128)S(1)}, f32[128]{0:T(128)}, u32[]{:S(2)}) copy-start(f32[128]{0:T(128)} %copy-done.21) | copy-start | bytes 1540
  498.0 3.1 copy-start.1
  511.0 3.2 copy-start.1
  524.0 3.2 copy-start.1
  537.0 3.2 copy-start.1
  550.1 3.2 copy-start.1
  563.1 3.2 copy-start.1
  576.1 3.2 copy-start.1
  589.2 3.2 copy-start.1
  (30 other events, 55.3 us)
Sparse Core Ops, SparseCore 0:
  12.0 97.6 all-gather.4
  113.7 88.9 all-gather.6
  235.1 58.7 reduce-scatter.1
  297.1 101.8 all-gather.8
  402.8 88.9 all-gather.10
where the time goes:
time: 610 us; the launch traced here: 608 us
  waiting for transfers between devices  194 us (32%)
  blocking collectives  171 us (28%)
  matrix products  158 us (26%)
  local copies, waits for them, and re-layouts  52.5 us (9%)
  other arithmetic  15.9 us (3%)
  between operations  14.8 us (2%)
    psum x1, blocking collectives, shards(): d_total = lax.psum(owned, 'ctx')  125 us
    all_gather x1, waiting for transfers between devices, shards(): lax.all_gather(key_rows, 'ctx', axis=0, tiled=True)  86.6 us
    all_gather x1, waiting for transfers between devices, shards(): grads_piece = lax.all_gather(d_rows, 'ctx', axis=0, tiled=True)  61 us
    all_gather x1, waiting for transfers between devices, shards(): lax.all_gather(value_rows, 'ctx', axis=0, tiled=True)  45.5 us
    dot_general x8, matrix products, inner_step(): jnp.einsum('hij,ihe->jhe', d_scores, query_blk, preferred_element_type=jn...  29.6 us
    dot_general x8, matrix products, query_step(): jnp.einsum('hij,jhe->ihe', d_scores, keys_blk, preferred_element_type=jnp...  26.8 us
    all_gather x1, blocking collectives, shards(): lax.all_gather(neg_unit.astype(jnp.bfloat16), 'batch', axis=0, tiled=True)  26.8 us
    dot_general x8, matrix products, inner_step(): jnp.einsum('hij,ihe->jhe', weights, grad_blk, preferred_element_type=jnp....  25.2 us
  transfers between devices with their start and end apart: 5, of which 3 were waited for; matrix products, arithmetic and copies ran while one was open for 12% of the time, Pallas kernels for 0%

commit v1 on v0

--- a/solution.py
+++ b/solution.py
@@ -1,3 +1,4 @@
+import functools
 import math
 import jax
 import jax.numpy as jnp
@@ -8,6 +9,15 @@
 HEAD = 64
 D = 512
 SOFTMAX_TEMPER = 0.05
+
+
+def meet_the_entries(v0, which_dim):
+    return jnp.concatenate(
+        lax.all_to_all(jnp.stack(lax.axis_size("ctx") * [v0]), "ctx", 0, 0), axis=which_dim
+    )
+
+
+_define_wall = functools.partial(meet_the_entries, which_dim=0)
 
 
 def silu_slope(scores):
@@ -42,7 +52,7 @@
     query_rows = proj[:, 2 * D : 3 * D]
     key_rows = proj[:, 3 * D :]
     all_values, all_keys = (
-        lax.all_gather(value_rows, "ctx", axis=0, tiled=True),
+        _define_wall(value_rows),
         lax.all_gather(key_rows, "ctx", axis=0, tiled=True),
     )
     length = all_keys.shape[0]

time: 610 us -> 560 us (0.918)
  waiting for transfers between devices: 194 us -> 115 us
  starting transfers between devices: 0.2 us -> 11.6 us
  blocking collectives: 171 us -> 181 us
  local copies, waits for them, and re-layouts: 52.5 us -> 60.7 us
    all_gather x1, waiting for transfers between devices: 86.6 us -> 2.96 us  [shards(): lax.all_gather(key_rows, 'ctx', axis=0, tiled=True)]
    all_to_all x0 -> x1, waiting for transfers between devices: none -> 49 us  [meet_the_entries(): lax.all_to_all(jnp.stack(lax.axis_size('ctx') * [v0]), 'ctx', 0, 0)]
    all_gather x1 -> x0, waiting for transfers between devices: 45.5 us -> none  [shards(): lax.all_gather(value_rows, 'ctx', axis=0, tiled=True)]
    all_to_all x0 -> x1, starting transfers between devices: none -> 11.4 us  [meet_the_entries(): lax.all_to_all(jnp.stack(lax.axis_size('ctx') * [v0]), 'ctx', 0, 0)]
    another operation x0 -> x2, local copies, waits for them, and re-layouts: none -> 10.2 us  [the longest x1 7.33 us: split_heads(): return matrix.reshape(matrix.shape[0], HEADS, HEAD)]
    all_to_all x0 -> x1, local copies, waits for them, and re-layouts: none -> 6.81 us  [meet_the_entries(): lax.all_to_all(jnp.stack(lax.axis_size('ctx') * [v0]), 'ctx', 0, 0)]
    all_gather x1 -> x0, local copies, waits for them, and re-layouts: 6.36 us -> none  [shards(): lax.all_gather(value_rows, 'ctx', axis=0, tiled=True)]
  transfers between devices with their start and end apart: 5 -> 5, of which waited for: 3 -> 3; matrix products, arithmetic and copies ran while one was open for 12% -> 14% of each run, Pallas kernels for 0% -> 0%
where the time goes in v1:
time: 560 us; the launch traced here: 558 us
  blocking collectives  181 us (32%)
  matrix products  158 us (28%)
  waiting for transfers between devices  115 us (21%)
  local copies, waits for them, and re-layouts  60.7 us (11%)
  other arithmetic  15.9 us (3%)
  between operations  14.8 us (3%)
  starting transfers between devices  11.6 us (2%)
    psum x1, blocking collectives, shards(): d_total = lax.psum(owned, 'ctx')  131 us
    all_gather x1, waiting for transfers between devices, shards(): grads_piece = lax.all_gather(d_rows, 'ctx', axis=0, tiled=True)  61.4 us
    all_to_all x1, waiting for transfers between devices, meet_the_entries(): lax.all_to_all(jnp.stack(lax.axis_size('ctx') * [v0]), 'ctx', 0, 0)  49 us
    dot_general x8, matrix products, inner_step(): jnp.einsum('hij,ihe->jhe', d_scores, query_blk, preferred_element_type=jn...  29.4 us
    all_gather x1, blocking collectives, shards(): lax.all_gather(neg_unit.astype(jnp.bfloat16), 'batch', axis=0, tiled=True)  28.7 us
    dot_general x8, matrix products, query_step(): jnp.einsum('hij,jhe->ihe', d_scores, keys_blk, preferred_element_type=jnp...  26.8 us
    dot_general x8, matrix products, inner_step(): jnp.einsum('hij,ihe->jhe', weights, grad_blk, preferred_element_type=jnp....  25.1 us
    dot_general x8, matrix products, query_step(): jnp.einsum('ihe,jhe->hij', d_heads, values_blk, preferred_element_type=jn...  23.5 us
  transfers between devices with their start and end apart: 5, of which 3 were waited for; matrix products, arithmetic and copies ran while one was open for 14% of the time, Pallas kernels for 0%

profile of v1, /device:TPU:1, one launch (start us, length us, event | category | flops | bytes accessed | tf_op | source)
XLA Modules:
  0.0 557.8 jit_solution(12414135449150090509)
XLA Ops:
  15.7 11.4 %all-to-all-start = ((bf16[32,128,512]{1,2,0:T(8,128)(2,1)}), bf16[32,128,512]{1,2,0:T(8,128)(2,1)}, u32[]{:S(2)}, u32[]{:S(2)}) async-start(bf16[32,128,512]{1,2,0:T(8,128)(2,1)} %stack.2), calls=%async_computation | async-start | bytes 8388608 | tf_op jit(solution)/shard_map/all_to_all | solution.py:16
  30.5 21.6 %all-reduce.2 = (s32[128]{0:T(128)S(1)}, s32[128]{0:T(128)}) all-reduce(s32[128]{0:T(128)S(1)} %dynamic-update-slice.1, s32[128]{0:T(128)S(1)} %dynamic-update-slice), channel_id=1, replica_groups=mesh['ctx'=32,'batch'=16] {'batch'}, use_global_device_ids=true, to_apply=%add.1 | all-reduce | flops 256 | bytes 2048
  52.3 28.7 %all_gather.20 = bf16[128,512]{1,0:T(8,128)(2,1)} all-gather(bf16[8,512]{1,0:T(8,128)(2,1)S(1)} %fusion.95), channel_id=1, replica_groups=mesh['ctx'=32,'batch'=16] {'batch'}, dimensions={0}, use_global_device_ids=true | all-gather | bytes 139264 | tf_op jit(solution)/shard_map/all_gather | solution.py:41
  83.4 49.0 %all-to-all-done = bf16[32,128,512]{1,2,0:T(8,128)(2,1)} async-done(((bf16[32,128,512]{1,2,0:T(8,128)(2,1)}), bf16[32,128,512]{1,2,0:T(8,128)(2,1)}, u32[]{:S(2)}, u32[]{:S(2)}) %all-to-all-start) | async-done | bytes 4194336 | tf_op jit(solution)/shard_map/all_to_all | solution.py:16
  132.4 6.8 %copy.45 = bf16[32,128,512]{1,0,2:T(8,128)(2,1)} copy(bf16[32,128,512]{1,2,0:T(8,128)(2,1)} %all-to-all-done) | data formatting | bytes 8388608 | tf_op jit(solution)/shard_map/all_to_all | solution.py:16
  139.2 7.3 %reshape_reshape.3 = bf16[4096,8,64]{0,2,1:T(8,128)(2,1)} reshape(bf16[32,128,512]{1,0,2:T(8,128)(2,1)} %copy.45) | data formatting | bytes 8388608 | tf_op jit(solution)/shard_map/reshape;reshape | solution.py:29
  149.5 6.4 %copy.46 = bf16[4096,512]{0,1:T(8,128)(2,1)} copy(bf16[4096,512]{1,0:T(8,128)(2,1)} %all-gather.4.cloned.1.call-done) | data formatting | bytes 8388608 | tf_op jit(solution)/shard_map/all_gather | solution.py:56
  155.8 19.7 %while.44 = (s32[]{:T(128)}, f32[128,8,64]{0,2,1:T(8,128)S(1)}, bf16[4096,8,64]{0,2,1:T(8,128)(2,1)}, bf16[4096,8,64]{0,2,1:T(8,128)(2,1)}, bf16[128,8,64]{0,2,1...) while((s32[]{:T(128)}, f32[128,8,64]{0,2,1:T(8,128)S(1)}, ...), condition=%wide.region_1.0_spmd.clone, body=%wide.region_0.0_spmd.clone.sunk | while | flops 138084992 | bytes 1841828 | solution.py:81
  188.9 57.4 %while.46 = (s32[]{:T(128)}, f32[128,8,64]{0,2,1:T(8,128)}, bf16[4096,8,64]{0,2,1:T(8,128)(2,1)}, bf16[4096,8,64]{0,2,1:T(8,128)(2,1)}, bf16[128,8,64]{0,2,1:T(8...) while((s32[]{:T(128)}, f32[128,8,64]{0,2,1:T(8,128)}, ...), condition=%wide.region_16.17_spmd.clone, body=%wide.region_15.16_spmd.clone.sunk | while | flops 207815296 | bytes 9313028 | solution.py:156
  192.0 3.3 fusion.161
  199.2 3.3 fusion.161
  206.4 3.4 fusion.161
  213.6 3.4 fusion.161
  220.7 3.4 fusion.161
  227.9 3.3 fusion.161
  235.1 3.3 fusion.161
  242.3 3.4 fusion.161
  248.7 131.0 %psum.7 = f32[8,512]{1,0:T(8,128)S(1)} all-reduce(bf16[8,512]{1,0:T(8,128)(2,1)} %reduce-scatter.2.cloned.1.call-done), channel_id=1, replica_groups=mesh['ctx'=32,'batch'=16] {'ctx'}, use_global_device_ids=true, to_apply=%region_18.19 | all-reduce | flops 4096 | bytes 24576 | tf_op jit(solution)/shard_map/psum | solution.py:119
  380.5 61.4 %all-gather.8.cloned.1.call-done = bf16[4096,512]{1,0:T(8,128)(2,1)} async-done(((bf16[128,512]{1,0:T(8,128)(2,1)}), bf16[4096,512]{1,0:T(8,128)(2,1)}) %all-gather.8.cloned.1.call-update) | async-done | bytes 4194320 | tf_op jit(solution)/shard_map/all_gather | solution.py:158
  441.9 104.2 %while.45 = (s32[]{:T(128)}, f32[128,8,64]{0,2,1:T(8,128)}, f32[128,8,64]{0,2,1:T(8,128)}, bf16[4096,512]{1,0:T(8,128)(2,1)}, bf16[4096,512]{1,0:T(8,128)(2,1)},...) while((s32[]{:T(128)}, f32[128,8,64]{0,2,1:T(8,128)}, ...), condition=%wide.region_14.15_spmd.clone, body=%wide.region_13.14_spmd.clone.sunk | while | flops 278725248 | bytes 16192726 | solution.py:187
  451.2 3.6 fusion.153
  461.1 3.1 fusion.154
  464.2 3.7 fusion.153
  474.1 3.1 fusion.154
  477.3 3.7 fusion.153
  490.3 3.7 fusion.153
  500.2 3.1 fusion.154
  503.3 3.7 fusion.153
  516.4 3.7 fusion.153
  526.3 3.1 fusion.154
  529.4 3.7 fusion.153
  542.4 3.7 fusion.153
  (292 shorter events, 149.7 us)
Async XLA Ops:
  12.6 15.3 %copy-start.4 = (bf16[128,512]{1,0:T(8,128)(2,1)}, bf16[128,512]{1,0:T(8,128)(2,1)S(1)}, u32[]{:S(2)}) copy-start(bf16[128,512]{1,0:T(8,128)(2,1)S(1)} %get-tuple-element.555) | copy-start | bytes 393220
  15.7 14.3 %copy-start.26 = (s32[8]{0:T(128)S(1)}, s32[8]{0:T(128)}, u32[]{:S(2)}) copy-start(s32[8]{0:T(128)} %param.20) | copy-start | bytes 100
  15.7 14.6 %copy-start.27 = (s32[8]{0:T(128)S(1)}, s32[8]{0:T(128)}, u32[]{:S(2)}) copy-start(s32[8]{0:T(128)} %param.21) | copy-start | bytes 100
  15.7 36.4 %copy-start.14 = (bf16[8,512]{1,0:T(8,128)(2,1)S(1)}, bf16[8,512]{1,0:T(8,128)(2,1)}, u32[]{:S(2)}) copy-start(bf16[8,512]{1,0:T(8,128)(2,1)} %param.19) | copy-start | bytes 24580
  15.7 65.9 %copy-start.3 = (bf16[1,128,512]{2,1,0:T(8,128)(2,1)S(1)}, bf16[1,128,512]{2,1,0:T(8,128)(2,1)}, u32[]{:S(2)}) copy-start(bf16[1,128,512]{2,1,0:T(8,128)(2,1)} %param.17) | copy-start | bytes 393220
  15.7 116.7 %all-to-all-start = ((bf16[32,128,512]{1,2,0:T(8,128)(2,1)}), bf16[32,128,512]{1,2,0:T(8,128)(2,1)}, u32[]{:S(2)}, u32[]{:S(2)}) async-start(bf16[32,128,512]{1,2,0:T(8,128)(2,1)} %stack.2), calls=%async_computation | async-start | bytes 8388608 | tf_op jit(solution)/shard_map/all_to_all | solution.py:16
  27.1 122.4 %all-gather.4.cloned.1.call-start = ((), (), s32[]{:S(2)}) async-start(), calls=%async_computation.2 | async-start | bytes 4325376 | tf_op jit(solution)/shard_map/all_gather | solution.py:56
  27.8 220.8 %reduce-scatter.2.cloned.1.call-start = ((), (), s32[]{:S(2)}) async-start(), calls=%async_computation.5 | async-start | bytes 139264 | tf_op jit(solution)/shard_map/reduce_scatter | solution.py:116
  52.2 87.0 %copy-start.18 = (f32[8]{0:T(128)}, f32[8]{0:T(128)S(1)}, u32[]{:S(2)}) copy-start(f32[8]{0:T(128)S(1)} %add_rsqrt_fusion) | copy-start | bytes 100
  155.8 20.5 %copy-start.2 = (bf16[512,512]{1,0:T(8,128)(2,1)S(1)}, bf16[512,512]{1,0:T(8,128)(2,1)}, u32[]{:S(2)}) copy-start(bf16[512,512]{1,0:T(8,128)(2,1)} %param.16) | copy-start | bytes 1572868
  178.6 5.0 copy-start.22
  180.2 3.4 copy-start.8
  181.7 198.8 %all-gather.6.cloned.1.call-start = ((), (), s32[]{:S(2)}) async-start(), calls=%async_computation.3 | async-start | bytes 4325376 | tf_op jit(solution)/shard_map/all_gather | solution.py:157
  182.5 259.4 %all-gather.8.cloned.1.call-start = ((), (), s32[]{:S(2)}) async-start(), calls=%async_computation.4 | async-start | bytes 4325376 | tf_op jit(solution)/shard_map/all_gather | solution.py:158
  185.0 3.2 copy-start.20
  188.9 59.3 %copy-start.23 = (f32[128]{0:T(128)S(1)}, f32[128]{0:T(128)}, u32[]{:S(2)}) copy-start(f32[128]{0:T(128)} %copy-done.22) | copy-start | bytes 1540
  188.9 59.3 %copy-start.25 = (f32[128]{0:T(128)S(1)}, f32[128]{0:T(128)}, u32[]{:S(2)}) copy-start(f32[128]{0:T(128)} %copy-done.24) | copy-start | bytes 1540
  188.9 190.7 %copy-start.19 = (f32[8]{0:T(128)S(1)}, f32[8]{0:T(128)}, u32[]{:S(2)}) copy-start(f32[8]{0:T(128)} %copy-done.18) | copy-start | bytes 100
  188.9 3.1 copy-start.10
  188.9 3.1 copy-start.13
  203.3 3.1 copy-start.13
  224.8 3.1 copy-start.13
  239.2 3.1 copy-start.13
  441.9 106.4 %copy-start.21 = (f32[128]{0:T(128)S(1)}, f32[128]{0:T(128)}, u32[]{:S(2)}) copy-start(f32[128]{0:T(128)} %copy-done.20) | copy-start | bytes 1540
  448.1 3.1 copy-start.1
  461.1 3.1 copy-start.1
  474.1 3.1 copy-start.1
  487.1 3.1 copy-start.1
  500.2 3.1 copy-start.1
  513.2 3.1 copy-start.1
  526.3 3.1 copy-start.1
  539.3 3.1 copy-start.1
  (29 other events, 53.9 us)
Sparse Core Ops, SparseCore 0:
  31.9 117.5 all-gather.3
  181.9 61.8 reduce-scatter.1
  247.1 101.9 all-gather.5
  352.9 88.8 all-gather.7
